TPU v7x, 32 devices: a whole 2x2x4 slice. The times are simulated.
32 devices in a mesh: ckpt: 4 (over z), shard: 8 (over y, x, core).
Axes of the slice: x: 2, y: 2, z: 4, core: 2. Of those that a mesh axis runs over, the one named last changes fastest.
Arguments:
- task_vectors: bfloat16 [4, 4096, 16384], P('ckpt', 'shard'), may hold values from -0.125 to 0.125, as said below
- thresholds: float32 [4], replicated, may hold values from 0.009 to 0.062, as said below
- base_weight: float32 [4096, 16384], P('ckpt', 'shard'), may hold values from -0.3 to 0.3
Outputs:
- merged: float32 [4096, 16384], P('ckpt', 'shard')
Inputs may be any that keep to these rules, and one draw needn't show every extreme that they name: `task_vectors`: every entry is a whole multiple of 2^-14. `thresholds`: every threshold is an odd multiple of 2^-15.
All inputs are finite; a program needn't handle non-finite values.
Results may differ from a plain program's by a relative error of at most 0.0003.
Values may be sent and summed in bfloat16 or wider, within the bound.
A program may use at most 128 MiB of HBM per device.

v0:
```python
import functools

import jax
import jax.numpy as jnp
from jax import lax
from jax.experimental import pallas as pl
from jax.experimental.pallas import tpu as pltpu
from jax.sharding import PartitionSpec as P

MESH = pl.DeviceIdType.MESH
VMEM_BYTES = 67043328
CHUNK = 16
AHEAD = 3
LAG = 4


def merge_kernel(
    T, S, R, cw,
    thr_ref, x_ref, base_ref, buf,
    stage, recv, thr,
    s1_send, s1_recv, s2_send, s2_recv, own_sem, base_sem, thr_sem,
):
    g = S // T
    RB, W = stage.shape[1], stage.shape[2]
    N = RB // R
    t = lax.axis_index("ckpt")
    s = lax.axis_index("shard")

    own = pltpu.make_async_copy(
        x_ref.at[0, :, pl.ds(pl.multiple_of(s * W, W), W)], stage.at[s], own_sem
    )
    base_in = pltpu.make_async_copy(base_ref, buf, base_sem)
    thr_in = pltpu.make_async_copy(thr_ref, thr, thr_sem)
    thr_in.start()
    own.start()
    base_in.start()

    barrier = pltpu.get_barrier_semaphore()
    for d in range(1, S):
        pl.semaphore_signal(
            barrier, inc=1, device_id=(t, lax.rem(s + d, S)), device_id_type=MESH
        )
    for d in range(1, T):
        pl.semaphore_signal(
            barrier, inc=1, device_id=(lax.rem(t + d, T), s), device_id_type=MESH
        )
    pl.semaphore_wait(barrier, S - 1 + T - 1)

    def rows_of(j):
        return pl.ds(pl.multiple_of(j * R, R), R)

    mine = lax.div(s, g)
    sign = 2 * lax.rem(mine, 2) - 1
    offsets = [(0, 0)]
    if T > 1:
        offsets.append((1, T // 2))
    for i in range(1, (T + 1) // 2):
        offsets += [(1, T - sign * i), (1, T + sign * i)]

    def plane_copy(j, e, q):
        c = lax.rem(mine + e[1], T) * g + lax.rem(lax.rem(s, g) + q, g)
        return pltpu.make_async_remote_copy(
            src_ref=x_ref.at[0, rows_of(j), pl.ds(pl.multiple_of(c * W, W), W)],
            dst_ref=stage.at[s, rows_of(j)],
            send_sem=s1_send.at[j],
            recv_sem=s1_recv.at[j, mine],
            device_id=(t, c),
            device_id_type=MESH,
        )

    def line_copy(j, k):
        return pltpu.make_async_remote_copy(
            src_ref=stage.at[pl.ds(k * g, g), rows_of(j)],
            dst_ref=recv.at[lax.rem(t - k - 1 + T, T), :, rows_of(j)],
            send_sem=s2_send.at[j],
            recv_sem=s2_recv.at[j],
            device_id=(k, s),
            device_id_type=MESH,
        )

    def plane_start(j):
        for e in offsets[1:] + offsets[:1]:
            for q in range(g):
                if e[0] or q:
                    plane_copy(j, e, q).start()

    def plane_arrived(j, e):
        count = g if e[0] else g - 1
        if count:
            part = stage.at[pl.ds(0, count), rows_of(j)]
            sem = s1_recv.at[j, lax.rem(mine + e[1], T)]
            pltpu.make_async_copy(part, part, sem).wait()

    def plane_sent(j):
        part = stage.at[pl.ds(0, S - 1), rows_of(j)]
        pltpu.make_async_copy(part, part, s1_send.at[j]).wait()

    def line_wait(sem, j):
        part = recv.at[:, :, rows_of(j)]
        pltpu.make_async_copy(part, part, sem.at[j]).wait()

    def mean_rows(j):
        limits = [thr[lax.rem(t + d, T)] for d in range(T)]
        rows = rows_of(j)

        def cols_step(q, carry):
            cols = pl.ds(pl.multiple_of(q * cw, cw), cw)
            for i in range(g):
                trimmed = []
                for d in range(T):
                    if d == 0:
                        v = stage[t * g + i, rows, cols]
                    else:
                        v = recv[d - 1, i, rows, cols]
                    v = v.astype(jnp.float32)
                    trimmed.append(jnp.where(jnp.abs(v) > limits[d], v, 0.0))
                total = functools.reduce(jnp.add, trimmed)
                kept = jnp.zeros_like(total)
                count = jnp.zeros_like(total)
                for v in trimmed:
                    agree = v * total > 0
                    kept = kept + jnp.where(agree, v, 0.0)
                    count = count + jnp.where(agree, 1.0, 0.0)
                buf[i, rows, cols] = buf[i, rows, cols] + kept / jnp.maximum(count, 1.0)
            return carry

        lax.fori_loop(0, W // cw, cols_step, 0)

    def finish(j):
        line_wait(s2_recv, j)
        mean_rows(j)

    ahead = min(AHEAD, N)
    for j in range(ahead):
        plane_start(j)
    own.wait()
    base_in.wait()
    thr_in.wait()

    def step(j, carry):
        @pl.when(j + ahead < N)
        def _():
            plane_start(j + ahead)

        for e in offsets:
            k = lax.rem(mine + e[1], T)
            plane_arrived(j, e)

            @pl.when(k != t)
            def _():
                line_copy(j, k).start()

        @pl.when(j >= LAG)
        def _():
            finish(j - LAG)

        return carry

    lax.fori_loop(0, N, step, 0)

    def tail(j, carry):
        finish(j)
        return carry

    lax.fori_loop(N - LAG, N, tail, 0)

    def drain(j, carry):
        plane_sent(j)
        line_wait(s2_send, j)
        return carry

    lax.fori_loop(0, N, drain, 0)


def local(task_vectors, thresholds, base_weight):
    T = lax.axis_size("ckpt")
    S = lax.axis_size("shard")
    RB = task_vectors.shape[1]
    W = task_vectors.shape[2] // S
    g = S // T
    R = min(CHUNK, RB)
    N = RB // R
    merged = pl.pallas_call(
        functools.partial(merge_kernel, T, S, R, min(W, 256)),
        out_shape=pltpu.VMEM((g, RB, W), jnp.float32),
        in_specs=[
            pl.BlockSpec(memory_space=pltpu.HBM),
            pl.BlockSpec(memory_space=pltpu.HBM),
            pl.BlockSpec(memory_space=pltpu.HBM),
        ],
        out_specs=pl.BlockSpec(memory_space=pltpu.VMEM),
        scratch_shapes=[
            pltpu.VMEM((S, RB, W), jnp.bfloat16),
            pltpu.VMEM((T - 1, g, RB, W), jnp.bfloat16),
            pltpu.SMEM((T,), jnp.float32),
            pltpu.SemaphoreType.DMA((N,)),
            pltpu.SemaphoreType.DMA((N, T)),
            pltpu.SemaphoreType.DMA((N,)),
            pltpu.SemaphoreType.DMA((N,)),
            pltpu.SemaphoreType.DMA,
            pltpu.SemaphoreType.DMA,
            pltpu.SemaphoreType.DMA,
        ],
        compiler_params=pltpu.CompilerParams(
            collective_id=0, has_side_effects=True, vmem_limit_bytes=VMEM_BYTES - g * RB * W * 4
        ),
        name="merge_exchange",
    )(thresholds, task_vectors, base_weight.reshape(g, RB, W))
    return merged.reshape(base_weight.shape)


def solution(mesh):
    placed = (P("ckpt", "shard", None), P(), P("ckpt", "shard"))
    return jax.shard_map(
        local, mesh=mesh, in_specs=placed, out_specs=P("ckpt", "shard"), check_vma=False
    )
```

profile of v0, /device:TPU:19, one launch (start us, length us, event | category | flops | bytes accessed | tf_op | source)
XLA Modules:
  0.0 375.8 jit_solution(18289959874635443275)
XLA Ops:
  0.0 372.4 %merge_exchange.1 = f32[2,512,2048]{2,1,0:T(8,128)S(1)} custom-call(f32[4]{0:T(128)} %thr_ref.1, bf16[1,512,16384]{2,1,0:T(8,128)(2,1)} %x_ref.1, f32[2,512,2048]{2,1,0:T(8,128)} %bitcast.3), custom_call_target="tpu_custom_call" | custom-call | tf_op jit(solution)/shard_map/merge_exchange/pallas_call | solution.py:183
  372.4 3.4 copy.5
where the time goes:
time: 376 us
  Pallas kernels  372 us (99%)
    pallas_call x1, Pallas kernels, local(): pl.pallas_call(functools.partial(merge_kernel, T, S, R, min(W, 256)), out...  372 us

commit v1 on v0

v1 whole, which is shorter than its diff:
```python
import functools

import jax
import jax.numpy as jnp
from jax import lax
from jax.experimental import pallas as pl
from jax.experimental.pallas import tpu as pltpu
from jax.sharding import PartitionSpec as P

MESH = pl.DeviceIdType.MESH
VMEM_BYTES = 67043328
EDGE_ROWS = 16
EDGE_COLS = 512
MAIN_ROWS = 32
AHEAD = 2
LAG = 2
BLOCK = (16, 256)


class Part:
    def __init__(self, first, rows, cols, width, height, sem):
        self.first, self.rows, self.cols = first, rows, cols
        self.across = width // cols
        self.count = self.across * (height // rows)
        self.sem = sem

    def tile(self, j):
        row = self.first + lax.div(j, self.across) * self.rows
        col = lax.rem(j, self.across) * self.cols
        return pl.multiple_of(row, self.rows if self.first % self.rows == 0 else 16), pl.multiple_of(col, self.cols)

    def at(self, j):
        row, col = self.tile(j)
        return pl.ds(row, self.rows), pl.ds(col, self.cols)


def split(RB, W):
    edge, cols = min(EDGE_ROWS, RB), min(EDGE_COLS, W)
    parts = [Part(0, edge, cols, W, edge, 0)]
    middle = RB - 2 * edge
    main = min(MAIN_ROWS, middle)
    parts.append(Part(edge, main, W, W, middle, parts[0].count))
    parts.append(Part(RB - edge, edge, cols, W, edge, parts[1].sem + parts[1].count))
    return parts


def merge_kernel(
    T, S,
    thr_ref, x_ref, base_ref, buf,
    stage, recv, thr,
    s1_send, s1_recv, s2_send, s2_recv, own_sem, base_sem, thr_sem,
):
    g = S // T
    RB, W = stage.shape[1], stage.shape[2]
    head, main, last = split(RB, W)
    t = lax.axis_index("ckpt")
    s = lax.axis_index("shard")
    mine = lax.div(s, g)
    sign = 2 * lax.rem(mine, 2) - 1
    steps = [0]
    if T > 1:
        steps.append(T // 2)
    for i in range(1, (T + 1) // 2):
        steps += [T - sign * i, T + sign * i]

    def own_copy(p, j):
        rows, cols = p.at(j)
        row, col = p.tile(j)
        src = pl.ds(pl.multiple_of(s * W + col, p.cols), p.cols)
        return pltpu.make_async_copy(x_ref.at[0, rows, src], stage.at[s, rows, cols], own_sem.at[p.sem + j])

    base_in = pltpu.make_async_copy(base_ref, buf, base_sem)
    thr_in = pltpu.make_async_copy(thr_ref, thr, thr_sem)

    def plane_copy(p, j, step, q):
        c = lax.rem(mine + step, T) * g + lax.rem(lax.rem(s, g) + q, g)
        rows, cols = p.at(j)
        row, col = p.tile(j)
        src = pl.ds(pl.multiple_of(c * W + col, p.cols), p.cols)
        return pltpu.make_async_remote_copy(
            src_ref=x_ref.at[0, rows, src],
            dst_ref=stage.at[s, rows, cols],
            send_sem=s1_send,
            recv_sem=s1_recv.at[p.sem + j, mine],
            device_id=(t, c),
            device_id_type=MESH,
        )

    def line_copy(p, j, k):
        rows, cols = p.at(j)
        return pltpu.make_async_remote_copy(
            src_ref=stage.at[pl.ds(k * g, g), rows, cols],
            dst_ref=recv.at[lax.rem(t - k - 1 + T, T), :, rows, cols],
            send_sem=s2_send,
            recv_sem=s2_recv.at[p.sem + j],
            device_id=(k, s),
            device_id_type=MESH,
        )

    def plane_start(p, j):
        for n, step in enumerate(steps[1:] + steps[:1]):
            for q in range(g):
                if n < T - 1 or q:
                    plane_copy(p, j, step, q).start()

    def plane_arrived(p, j, k):
        rows, cols = p.at(j)
        sem = s1_recv.at[p.sem + j, k]
        if g > 1:
            @pl.when(k == mine)
            def _():
                part = stage.at[pl.ds(0, g - 1), rows, cols]
                pltpu.make_async_copy(part, part, sem).wait()

        @pl.when(k == mine)
        def _():
            own_copy(p, j).wait()

        @pl.when(k != mine)
        def _():
            part = stage.at[pl.ds(0, g), rows, cols]
            pltpu.make_async_copy(part, part, sem).wait()

    def order(n):
        half = max(T // 2, 1)
        other = jnp.where(2 * t < T, T - half, 0)
        if n < half:
            return other + lax.rem(mine + n, half)
        return lax.rem(other + half, T) + lax.rem(mine + n, half)

    def line_start(p, j):
        for n in range(T):
            k = order(n)
            plane_arrived(p, j, k)

            @pl.when(k != t)
            def _():
                line_copy(p, j, k).start()

    def mean_tile(p, j):
        limits = [thr[lax.rem(t + d, T)] for d in range(T)]
        row, col = p.tile(j)
        br, bc = min(BLOCK[0], p.rows), min(BLOCK[1], p.cols)
        across = p.cols // bc

        def block(n, carry):
            rows = pl.ds(pl.multiple_of(row + lax.div(n, across) * br, br), br)
            cols = pl.ds(pl.multiple_of(col + lax.rem(n, across) * bc, bc), bc)
            for i in range(g):
                trimmed = []
                for d in range(T):
                    if d == 0:
                        v = stage[t * g + i, rows, cols]
                    else:
                        v = recv[d - 1, i, rows, cols]
                    v = v.astype(jnp.float32)
                    trimmed.append(jnp.where(jnp.abs(v) > limits[d], v, 0.0))
                total = functools.reduce(jnp.add, trimmed)
                kept = jnp.zeros_like(total)
                count = jnp.zeros_like(total)
                for v in trimmed:
                    agree = v * total > 0
                    kept = kept + jnp.where(agree, v, 0.0)
                    count = count + jnp.where(agree, 1.0, 0.0)
                buf[i, rows, cols] = buf[i, rows, cols] + kept / jnp.maximum(count, 1.0)
            return carry

        lax.fori_loop(0, (p.rows // br) * across, block, 0)

    def finish(p, j):
        rows, cols = p.at(j)
        part = recv.at[:, :, rows, cols]
        pltpu.make_async_copy(part, part, s2_recv.at[p.sem + j]).wait()
        mean_tile(p, j)

    def loop(p, body, start=0, stop=None):
        def step(j, carry):
            body(p, j)
            return carry

        lax.fori_loop(start, p.count if stop is None else stop, step, 0)

    def send_plane(p, j):
        own_copy(p, j).start()
        plane_start(p, j)

    def own_start(p, j):
        own_copy(p, j).start()

    thr_in.start()
    loop(head, own_start)

    barrier = pltpu.get_barrier_semaphore()
    for d in range(1, S):
        pl.semaphore_signal(
            barrier, inc=1, device_id=(t, lax.rem(s + d, S)), device_id_type=MESH
        )
    for d in range(1, T):
        pl.semaphore_signal(
            barrier, inc=1, device_id=(lax.rem(t + d, T), s), device_id_type=MESH
        )
    pl.semaphore_wait(barrier, S - 1 + T - 1)

    ahead = min(AHEAD, main.count)
    lag = min(LAG, main.count)
    loop(head, plane_start)
    loop(main, send_plane, 0, ahead)
    base_in.start()
    loop(head, line_start)

    def step(p, j):
        @pl.when(j + ahead < p.count)
        def _():
            send_plane(p, j + ahead)

        @pl.when(j + ahead == p.count)
        def _():
            loop(last, send_plane)

        line_start(p, j)

        @pl.when(j + 1 == lag)
        def _():
            base_in.wait()
            thr_in.wait()
            loop(head, finish)

        @pl.when(j >= lag)
        def _():
            finish(p, j - lag)

    loop(main, step)
    loop(last, line_start)
    loop(main, finish, main.count - lag)
    loop(last, finish)

    part = stage.at[pl.ds(0, S - 1)]
    pltpu.make_async_copy(part, part, s1_send).wait()
    pltpu.make_async_copy(recv, recv, s2_send).wait()


def local(task_vectors, thresholds, base_weight):
    T = lax.axis_size("ckpt")
    S = lax.axis_size("shard")
    RB = task_vectors.shape[1]
    W = task_vectors.shape[2] // S
    g = S // T
    N = sum(p.count for p in split(RB, W))
    merged = pl.pallas_call(
        functools.partial(merge_kernel, T, S),
        out_shape=pltpu.VMEM((g, RB, W), jnp.float32),
        in_specs=[
            pl.BlockSpec(memory_space=pltpu.HBM),
            pl.BlockSpec(memory_space=pltpu.HBM),
            pl.BlockSpec(memory_space=pltpu.HBM),
        ],
        out_specs=pl.BlockSpec(memory_space=pltpu.VMEM),
        scratch_shapes=[
            pltpu.VMEM((S, RB, W), jnp.bfloat16),
            pltpu.VMEM((T - 1, g, RB, W), jnp.bfloat16),
            pltpu.SMEM((T,), jnp.float32),
            pltpu.SemaphoreType.DMA,
            pltpu.SemaphoreType.DMA((N, T)),
            pltpu.SemaphoreType.DMA,
            pltpu.SemaphoreType.DMA((N,)),
            pltpu.SemaphoreType.DMA((N,)),
            pltpu.SemaphoreType.DMA,
            pltpu.SemaphoreType.DMA,
        ],
        compiler_params=pltpu.CompilerParams(
            collective_id=0, has_side_effects=True, vmem_limit_bytes=VMEM_BYTES - g * RB * W * 4
        ),
        name="merge_exchange",
    )(thresholds, task_vectors, base_weight.reshape(g, RB, W))
    return merged.reshape(base_weight.shape)


def solution(mesh):
    placed = (P("ckpt", "shard", None), P(), P("ckpt", "shard"))
    return jax.shard_map(
        local, mesh=mesh, in_specs=placed, out_specs=P("ckpt", "shard"), check_vma=False
    )
```

time: 376 us -> 374 us (level)
  no operation moved by 1% of the time
where the time goes in v1:
time: 374 us; the launch traced here: 373 us
  Pallas kernels  370 us (99%)
    pallas_call x1, Pallas kernels, local(): pl.pallas_call(functools.partial(merge_kernel, T, S), out_shape=pltpu.VME...  370 us

profile of v1, /device:TPU:19, one launch (start us, length us, event | category | flops | bytes accessed | tf_op | source)
XLA Modules:
  0.0 373.4 jit_solution(2867427638736427032)
XLA Ops:
  0.0 370.0 %merge_exchange.1 = f32[2,512,2048]{2,1,0:T(8,128)S(1)} custom-call(f32[4]{0:T(128)} %thr_ref.1, bf16[1,512,16384]{2,1,0:T(8,128)(2,1)} %x_ref.1, f32[2,512,2048]{2,1,0:T(8,128)} %bitcast.3), custom_call_target="tpu_custom_call" | custom-call | tf_op jit(solution)/shard_map/merge_exchange/pallas_call | solution.py:249
  370.0 3.4 copy.5

commit v2 on v1

--- a/solution.py
+++ b/solution.py
@@ -10,10 +10,11 @@
 MESH = pl.DeviceIdType.MESH
 VMEM_BYTES = 67043328
 EDGE_ROWS = 16
-EDGE_COLS = 512
+EDGE_COLS = 256
+RAMP = 2
 MAIN_ROWS = 32
-AHEAD = 2
-LAG = 2
+AHEAD = 4
+LAG = 5
 BLOCK = (16, 256)
 
 
@@ -36,11 +37,16 @@
 
 def split(RB, W):
     edge, cols = min(EDGE_ROWS, RB), min(EDGE_COLS, W)
-    parts = [Part(0, edge, cols, W, edge, 0)]
-    middle = RB - 2 * edge
-    main = min(MAIN_ROWS, middle)
-    parts.append(Part(edge, main, W, W, middle, parts[0].count))
-    parts.append(Part(RB - edge, edge, cols, W, edge, parts[1].sem + parts[1].count))
+    middle = RB - (2 + RAMP) * edge
+    parts, row, sem = [], 0, 0
+    for rows, wide, height in (
+        (edge, cols, edge),
+        (edge, W, RAMP * edge),
+        (min(MAIN_ROWS, middle), W, middle),
+        (edge, cols, edge),
+    ):
+        parts.append(Part(row, rows, wide, W, height, sem))
+        row, sem = row + height, sem + parts[-1].count
     return parts
 
 
@@ -48,11 +54,11 @@
     T, S,
     thr_ref, x_ref, base_ref, buf,
     stage, recv, thr,
-    s1_send, s1_recv, s2_send, s2_recv, own_sem, base_sem, thr_sem,
+    s1_send, s1_recv, s2_send, s2_recv, own_sem, base_sem, thr_sem, half_in, all_in,
 ):
     g = S // T
     RB, W = stage.shape[1], stage.shape[2]
-    head, main, last = split(RB, W)
+    head, ramp, main, last = split(RB, W)
     t = lax.axis_index("ckpt")
     s = lax.axis_index("shard")
     mine = lax.div(s, g)
@@ -121,16 +127,20 @@
             part = stage.at[pl.ds(0, g), rows, cols]
             pltpu.make_async_copy(part, part, sem).wait()
 
+    half = T // 2
+    low = 2 * t < T
+    inner, outer = jnp.where(low, t + 1, t - 1), jnp.where(low, t - 1, t + 1)
+    depth = jnp.where(low, t, T - 1 - t)
+
     def order(n):
-        half = max(T // 2, 1)
-        other = jnp.where(2 * t < T, T - half, 0)
+        other = jnp.where(low, half, 0)
         if n < half:
             return other + lax.rem(mine + n, half)
-        return lax.rem(other + half, T) + lax.rem(mine + n, half)
-
-    def line_start(p, j):
-        for n in range(T):
-            k = order(n)
+        return half - other + lax.rem(mine + n, half)
+
+    def line_start(p, j, ns=range(T)):
+        for n in ns:
+            k = order(n) if p is head else jnp.where(low, T - 1 - n, n)
             plane_arrived(p, j, k)
 
             @pl.when(k != t)
@@ -191,22 +201,54 @@
     loop(head, own_start)
 
     barrier = pltpu.get_barrier_semaphore()
+
+    def tell(sem, k):
+        pl.semaphore_signal(sem, inc=1, device_id=(k, s), device_id_type=MESH)
+
     for d in range(1, S):
         pl.semaphore_signal(
             barrier, inc=1, device_id=(t, lax.rem(s + d, S)), device_id_type=MESH
         )
-    for d in range(1, T):
-        pl.semaphore_signal(
-            barrier, inc=1, device_id=(lax.rem(t + d, T), s), device_id_type=MESH
-        )
-    pl.semaphore_wait(barrier, S - 1 + T - 1)
+
+    @pl.when(depth == half - 1)
+    def _():
+        tell(barrier, inner)
+
+    @pl.when(depth > 0)
+    def _():
+        tell(barrier, outer)
+
+    pl.semaphore_wait(barrier, S)
+
+    def met():
+        @pl.when(depth > 0)
+        def _():
+            pl.semaphore_wait(half_in, 1)
+
+        @pl.when(depth < half - 1)
+        def _():
+            tell(half_in, inner)
+            pl.semaphore_wait(all_in, 1)
+
+        @pl.when(depth == half - 1)
+        def _():
+            tell(all_in, inner)
+            pl.semaphore_wait(all_in, 1)
+
+        @pl.when(depth > 0)
+        def _():
+            tell(all_in, outer)
 
     ahead = min(AHEAD, main.count)
     lag = min(LAG, main.count)
     loop(head, plane_start)
+    loop(ramp, send_plane)
     loop(main, send_plane, 0, ahead)
+    met()
+    loop(head, functools.partial(line_start, ns=range(half)))
+    loop(head, functools.partial(line_start, ns=range(half, T)))
     base_in.start()
-    loop(head, line_start)
+    loop(ramp, line_start)
 
     def step(p, j):
         @pl.when(j + ahead < p.count)
@@ -224,13 +266,15 @@
             base_in.wait()
             thr_in.wait()
             loop(head, finish)
+            loop(ramp, finish)
 
         @pl.when(j >= lag)
         def _():
             finish(p, j - lag)
 
     loop(main, step)
-    loop(last, line_start)
+    loop(last, functools.partial(line_start, ns=range(1)))
+    loop(last, functools.partial(line_start, ns=range(1, T)))
     loop(main, finish, main.count - lag)
     loop(last, finish)
 
@@ -266,6 +310,8 @@
             pltpu.SemaphoreType.DMA((N,)),
             pltpu.SemaphoreType.DMA,
             pltpu.SemaphoreType.DMA,
+            pltpu.SemaphoreType.REGULAR,
+            pltpu.SemaphoreType.REGULAR,
         ],
         compiler_params=pltpu.CompilerParams(
             collective_id=0, has_side_effects=True, vmem_limit_bytes=VMEM_BYTES - g * RB * W * 4

time: 374 us -> 373 us (level)
  no operation moved by 1% of the time
where the time goes in v2:
time: 373 us; the launch traced here: 372 us
  Pallas kernels  369 us (99%)
    pallas_call x1, Pallas kernels, local(): pl.pallas_call(functools.partial(merge_kernel, T, S), out_shape=pltpu.VME...  369 us

profile of v2, /device:TPU:19, one launch (start us, length us, event | category | flops | bytes accessed | tf_op | source)
XLA Modules:
  0.0 372.4 jit_solution(17342874949385850440)
XLA Ops:
  0.0 369.0 %merge_exchange.1 = f32[2,512,2048]{2,1,0:T(8,128)S(1)} custom-call(f32[4]{0:T(128)} %thr_ref.1, bf16[1,512,16384]{2,1,0:T(8,128)(2,1)} %x_ref.1, f32[2,512,2048]{2,1,0:T(8,128)} %bitcast.3), custom_call_target="tpu_custom_call" | custom-call | tf_op jit(solution)/shard_map/merge_exchange/pallas_call | solution.py:293
  369.0 3.4 copy.5
